TPU v7x, 32 devices: a whole 2x2x4 slice. The times are simulated.
32 devices in a mesh: tm: 8 (over y, x, core), lane: 4 (over z).
Axes of the slice: x: 2, y: 2, z: 4, core: 2. Of those that a mesh axis runs over, the one named last changes fastest.
Arguments:
- replay: bfloat16 [4, 8, 1024, 1024], P('lane', 'tm'), may hold values from -6 to 6
- block_owner: int32 [8, 4, 8, 1], P('tm'), may hold values from 0 to 3; in each aligned block of 8 rows (0 to 7, 8 to 15, ..., all dimensions but the last counted through in order) at most 2 rows name the same one
- block_slot: int32 [8, 4, 8], P('tm'), may hold values from 0 to 3
- block_fill: int32 [4, 8, 8], P('lane', 'tm'), may hold values from 64 to 256
- log_decay: float32 [4, 16, 16384], P('lane', None, 'tm'), may hold values from -2 to 0
- resets: int32 [4, 16384], P('lane', 'tm'), may hold values from 0 to 1, as said below
- cotangent: bfloat16 [4, 16384, 1024], P('lane', 'tm'), may hold values from -6 to 6
- w_in: bfloat16 [1024, 1024], replicated, may hold values from -0.1875 to 0.1875
- w_bc: bfloat16 [1024, 128], replicated, may hold values from -0.01171875 to 0.01171875
- w_out: bfloat16 [1024, 1024], replicated, may hold values from -0.1875 to 0.1875
Outputs:
- grad_in: float32 [1024, 1024], P(('tm', 'lane'))
- grad_bc: float32 [1024, 128], P(('tm', 'lane'))
- grad_out: float32 [1024, 1024], P(('tm', 'lane'))
Inputs may be any that keep to these rules, and one draw needn't show every extreme that they name: `block_owner`: among the 8 blocks of one segment on one time shard, no owner is named more than 2 times. `resets`: exactly one step of each segment is flagged.
All inputs are finite; a program needn't handle non-finite values.
Results may differ from a plain program's by a relative error of at most 0.0057.
Values may be sent and summed in bfloat16 or wider, within the bound.
A program may use at most 192 MiB of HBM per device.

v0:
```python
import math

import jax
import jax.numpy as jnp
from jax import lax
from jax.sharding import PartitionSpec as P

D = 1024
HEAD = 64
STATE = 64
BLOCK = 256
BUFCH = 4
TOK_DEV = 2048


def carried_in_2(value, axis, join, neutral, backward):
    count, mine = (lax.axis_size(axis), lax.axis_index(axis))
    pieces = jax.tree.map(lambda part: lax.all_gather(part, axis), value)
    if backward:
        pieces = jax.tree.map(lambda part: part[::-1], pieces)
        mine = count - 1 - mine
    subtotal = jax.tree.map(
        lambda part, zero: jnp.full_like(part, 0) + jnp.asarray(zero, part.dtype), value, neutral
    )

    def hop(position, subtotal):
        longer = join(subtotal, jax.tree.map(lambda part: part[position], pieces))
        return jax.tree.map(lambda new, old: jnp.where(position < mine, new, old), longer, subtotal)

    return lax.fori_loop(0, count - 1, hop, subtotal)


def decay_matrix(log_rate, episode_flags):
    cumulated = jnp.cumsum(log_rate, axis=1)
    counted = jnp.cumsum(episode_flags)
    extent = log_rate.shape[1]
    row_pos = lax.broadcasted_iota(jnp.int32, (extent, extent), 0)
    col_pos = lax.broadcasted_iota(jnp.int32, (extent, extent), 1)
    linked = (counted[:, None] == counted[None, :]) & (col_pos <= row_pos)
    spread = jnp.where(linked[None], cumulated[:, :, None] - cumulated[:, None, :], 0.0)
    return jnp.where(linked[None], jnp.exp(spread), 0.0)


def edge_weights(log_rate, episode_flags):
    cumulated = jnp.cumsum(log_rate, axis=1)
    counted = jnp.cumsum(episode_flags)
    opening = jnp.where(counted[None, :] == 0, jnp.exp(cumulated), 0.0)
    closing = jnp.where(
        counted[None, :] == counted[-1], jnp.exp(cumulated[:, -1:] - cumulated), 0.0
    )
    return (opening, closing)


def product(spec, left_op, right_op):
    return jnp.einsum(spec, left_op, right_op, preferred_element_type=jnp.float32)


def block_grads(block_items):
    (
        inner_proj,
        write_keys,
        read_keys,
        upstream,
        log_rate,
        episode_flags,
        opening,
        closing,
        weighted_in,
        weighted_out,
        start_state,
        end_adjoint,
    ) = block_items
    extent = inner_proj.shape[0]
    decays = decay_matrix(log_rate, episode_flags)
    scores = lax.dot_general(
        read_keys, write_keys, (((1,), (1,)), ((), ())), preferred_element_type=jnp.float32
    )
    mixing = (decays * scores[None]).astype(jnp.bfloat16)
    state_bf = start_state.astype(jnp.bfloat16)
    adjoint_bf = end_adjoint.astype(jnp.bfloat16)
    carried = product("in,hpn->ihp", read_keys, state_bf)
    readout = product("hij,jhp->ihp", mixing, inner_proj) + opening.T[:, :, None] * carried
    pairing = product("ihp,jhp->hij", upstream, inner_proj)
    blended = (decays * pairing).astype(jnp.bfloat16)
    returned = product("jn,hpn->jhp", write_keys, adjoint_bf)
    grad_inner = product("hij,ihp->jhp", mixing, upstream) + closing.T[:, :, None] * returned
    grad_write = product("hij,in->jn", blended, read_keys) + product(
        "jhp,hpn->jn", weighted_in, adjoint_bf
    )
    grad_read = product("hij,jn->in", blended, write_keys) + product(
        "ihp,hpn->in", weighted_out, state_bf
    )
    return (
        readout.astype(jnp.bfloat16).reshape(extent, -1),
        grad_inner.astype(jnp.bfloat16).reshape(extent, -1),
        jnp.concatenate([grad_write, grad_read], axis=1).astype(jnp.bfloat16),
    )


def advance(carried_in, block_items):
    current, gained = carried_in
    block_factor, pushed = block_items
    return (
        (block_factor[:, None, None] * current + pushed, gained * block_factor),
        (current, gained),
    )


def combine(former, latter):
    return (former[0] * latter[0], latter[0][:, None, None] * former[1] + latter[1])


def on_device(
    replay, block_owner, block_slot, block_fill, log_decay, resets, cotangent, w_in, w_bc, w_out
):
    lane_count = lax.axis_size("lane")
    shards = lax.axis_size("tm")
    my_lane = lax.axis_index("lane")
    num_heads = D // HEAD
    blocks = block_fill.shape[2]
    owners = block_owner[0, :, :, 0]
    slot_map = block_slot[0]
    my_owner = lax.dynamic_index_in_dim(owners, my_lane, 0, keepdims=False)
    capacity = max(2, (blocks + lane_count - 1) // lane_count)
    order_pos = lax.broadcasted_iota(jnp.int32, (blocks, blocks), 0)
    other_pos = lax.broadcasted_iota(jnp.int32, (blocks, blocks), 1)
    ranking = jnp.sum(
        ((owners[:, :, None] == owners[:, None, :]) & (other_pos < order_pos)[None]).astype(
            jnp.int32
        ),
        axis=2,
    )
    slot_ids = lax.broadcasted_iota(jnp.int32, (lane_count, capacity, blocks), 1)
    picked = (owners[:, None, :] == my_lane) & (ranking[:, None, :] == slot_ids)
    buffer_ids = lax.broadcasted_iota(jnp.int32, (lane_count, capacity, blocks, BUFCH), 3)
    selector = jnp.any(picked[..., None] & (slot_map[:, None, :, None] == buffer_ids), axis=2)
    stored = replay.reshape(BUFCH, BLOCK * D)
    outgoing = jnp.dot(
        selector.reshape(lane_count * capacity, BUFCH).astype(jnp.bfloat16),
        stored,
        preferred_element_type=jnp.float32,
    ).astype(jnp.bfloat16)
    received = lax.all_to_all(
        outgoing.reshape(lane_count, capacity * BLOCK * D),
        "lane",
        split_axis=0,
        concat_axis=0,
        tiled=True,
    )
    my_rank = lax.dynamic_index_in_dim(ranking, my_lane, 0, keepdims=False)
    source_ids = lax.broadcasted_iota(jnp.int32, (blocks, lane_count * capacity), 1)
    placing = (source_ids == (my_owner * capacity + my_rank)[:, None]).astype(jnp.bfloat16)
    delivered = jnp.dot(
        placing,
        received.reshape(lane_count * capacity, BLOCK * D),
        preferred_element_type=jnp.float32,
    ).astype(jnp.bfloat16)
    usable = (
        lax.broadcasted_iota(jnp.int32, (blocks, BLOCK), 1) < block_fill[0, 0][:, None]
    ).reshape(blocks * BLOCK)
    delivered = jnp.where(
        usable[:, None], delivered.reshape(blocks * BLOCK, D), jnp.zeros((), jnp.bfloat16)
    )
    masked = jnp.where(usable[:, None], cotangent[0], jnp.zeros((), jnp.bfloat16))
    inner_proj = jnp.dot(delivered, w_in, preferred_element_type=jnp.float32).astype(jnp.bfloat16)
    projected = jnp.dot(delivered, w_bc, preferred_element_type=jnp.float32).astype(jnp.bfloat16)
    upstream = lax.dot_general(
        masked, w_out, (((1,), (1,)), ((), ())), preferred_element_type=jnp.float32
    ).astype(jnp.bfloat16)
    inner_b = inner_proj.reshape(blocks, BLOCK, num_heads, HEAD)
    upstream_b = upstream.reshape(blocks, BLOCK, num_heads, HEAD)
    write_b = projected[:, :STATE].reshape(blocks, BLOCK, STATE)
    read_b = projected[:, STATE:].reshape(blocks, BLOCK, STATE)
    rates_b = jnp.transpose(log_decay[0].reshape(num_heads, blocks, BLOCK), (1, 0, 2))
    flags_b = resets[0].reshape(blocks, BLOCK)
    opening, closing = jax.vmap(edge_weights)(rates_b, flags_b)
    factor = opening[:, :, -1]
    weighted_in = (jnp.transpose(closing, (0, 2, 1))[..., None] * inner_b).astype(jnp.bfloat16)
    weighted_out = (jnp.transpose(opening, (0, 2, 1))[..., None] * upstream_b).astype(jnp.bfloat16)
    push_fwd = product("kjhp,kjn->khpn", weighted_in, write_b)
    push_bwd = product("kihp,kin->khpn", weighted_out, read_b)
    zero_state = jnp.zeros((num_heads, HEAD, STATE), jnp.float32)
    unit_gain = jnp.ones((num_heads,), jnp.float32)
    (dev_state, dev_gain), (local_start, prefix_gain) = lax.scan(
        advance, (zero_state, unit_gain), (factor, push_fwd)
    )
    (dev_back, dev_gain_back), (local_end, suffix_gain) = lax.scan(
        advance, (zero_state, unit_gain), (factor, push_bwd), reverse=True
    )
    enter_state = carried_in_2(
        (dev_gain, dev_state), "tm", combine, (unit_gain, zero_state), False
    )[1]
    enter_adjoint = carried_in_2(
        (dev_gain_back, dev_back), "tm", combine, (unit_gain, zero_state), True
    )[1]
    starts = local_start + prefix_gain[:, :, None, None] * enter_state
    ends = local_end + suffix_gain[:, :, None, None] * enter_adjoint
    readout, grad_inner, grad_keys = lax.map(
        block_grads,
        (
            inner_b,
            write_b,
            read_b,
            upstream_b,
            rates_b,
            flags_b,
            opening,
            closing,
            weighted_in,
            weighted_out,
            starts,
            ends,
        ),
    )
    readout = readout.reshape(blocks * BLOCK, D)
    grad_inner = grad_inner.reshape(blocks * BLOCK, D)
    grad_keys = grad_keys.reshape(blocks * BLOCK, 2 * STATE)
    grad_scale = 1.0 / math.sqrt(TOK_DEV * shards * lane_count)
    contract = (((0,), (0,)), ((), ()))
    summed = lax.psum_scatter(
        jnp.concatenate(
            [
                lax.dot_general(
                    delivered, grad_inner, contract, preferred_element_type=jnp.float32
                ),
                lax.dot_general(delivered, grad_keys, contract, preferred_element_type=jnp.float32),
                lax.dot_general(readout, masked, contract, preferred_element_type=jnp.float32),
            ],
            axis=1,
        )
        * grad_scale,
        ("tm", "lane"),
        scatter_dimension=0,
        tiled=True,
    )
    return (summed[:, :D], summed[:, D : D + 2 * STATE], summed[:, D + 2 * STATE :])


def solution(mesh):
    placed = (
        P("lane", "tm", None, None),
        P("tm", None, None, None),
        P("tm", None, None),
        P("lane", "tm", None),
        P("lane", None, "tm"),
        P("lane", "tm"),
        P("lane", "tm", None),
        P(),
        P(),
        P(),
    )
    return jax.shard_map(
        on_device,
        mesh=mesh,
        in_specs=placed,
        out_specs=(P(("tm", "lane"), None), P(("tm", "lane"), None), P(("tm", "lane"), None)),
        check_vma=False,
    )
```

profile of v0, /device:TPU:0, one launch (start us, length us, event | category | flops | bytes accessed | tf_op | source)
XLA Modules:
  0.0 740.8 jit_solution(15567319304836043288)
XLA Ops:
  9.9 4.6 reshape.334
  14.5 4.8 convolution_convert_fusion.1
  19.3 11.6 %all_to_all.8 = bf16[4,1,524288]{2,1,0:T(2,128)(2,1)} reshape(bf16[8,262144]{1,0:T(8,128)(2,1)} %convolution_convert_fusion.1) | data formatting | bytes 8388608 | tf_op jit(solution)/shard_map/all_to_all | solution.py:143
  31.4 29.0 %reduce.17 = bf16[4,524288]{1,0:T(4,128)(2,1)} reduce(bf16[4,1,524288]{2,1,0:T(2,128)(2,1)} %all_to_all.8, bf16[]{:T(256)} %broadcast.198), dimensions={1}, to_apply=%all_to_all.8.reduce_sub_computation | reduce | bytes 8388610 | tf_op jit(solution)/shard_map/all_to_all | solution.py:143
  60.4 8.3 %reshape.387 = bf16[4,2,262144]{2,1,0:T(2,128)(2,1)} reshape(bf16[4,524288]{1,0:T(4,128)(2,1)} %reduce.17) | data formatting | bytes 8388608
  68.7 6.5 all-to-all-start
  78.6 4.6 reduce-window.31
  86.5 8.6 %fusion.74 = bf16[2048,1024]{1,0:T(8,128)(2,1)} fusion(bf16[1024,1024]{1,0:T(8,128)(2,1)S(1)} %copy-done, bf16[1,2048,1024]{2,1,0:T(8,128)(2,1)} %param.26, pred[2048]{0:T(1024)(128)(4,1)} %lt.84), kind=kOutput, calls=%fused_computation.115 | convolution fusion | flops 4299161600 | bytes 10487808 | tf_op jit(solution)/shard_map/dot_general | solution.py:167
  95.0 6.5 copy.174
  101.5 5.7 copy.219
  108.1 5.0 multiply_convert_fusion.8
  113.1 55.5 %all-to-all-done = bf16[4,2,262144]{2,1,0:T(2,128)(2,1)} async-done(((bf16[4,2,262144]{2,1,0:T(2,128)(2,1)}), bf16[4,2,262144]{2,1,0:T(2,128)(2,1)}, u32[]{:S(2)}, u32[]{:S(2)}) %all-to-all-start) | async-done | bytes 4194336 | tf_op jit(solution)/shard_map/all_to_all | solution.py:143
  168.6 7.4 %reshape.388 = bf16[4,1,524288]{2,1,0:T(2,128)(2,1)} reshape(bf16[4,2,262144]{2,1,0:T(2,128)(2,1)} %all-to-all-done) | data formatting | bytes 8388608
  176.0 28.2 %reduce.2 = bf16[4,524288]{1,0:T(4,128)(2,1)} reduce(bf16[4,1,524288]{2,1,0:T(2,128)(2,1)} %reshape.388, bf16[]{:T(256)} %constant.194), dimensions={1}, to_apply=%all_to_all.7.reduce_sub_computation | reduce | bytes 8388610 | tf_op jit(solution)/shard_map/all_to_all | solution.py:143
  204.2 5.2 reshape.335
  210.8 6.7 broadcast_select_fusion.3
  217.6 6.2 reshape.336
  223.8 8.6 %convolution_convert_fusion.2 = bf16[2048,1024]{1,0:T(8,128)(2,1)} fusion(bf16[1024,1024]{1,0:T(8,128)(2,1)S(1)} %copy-done.22, bf16[2048,1024]{1,0:T(8,128)(2,1)} %reshape.336, pred[2048]{0:T(1024)(128)(4,1)S(1)} %copy-done.18), kind=kOutput, calls=%fused_computation.116 | convolution fusion | flops 4299161600 | bytes 10487808 | tf_op jit(solution)/shard_map/dot_general | solution.py:165
  232.3 6.5 copy.165
  238.9 3.8 copy.216
  245.9 3.2 fusion.79
  251.6 16.6 %while.81 = (s32[]{:T(128)}, f32[16,64,64]{2,1,0:T(8,128)S(1)}, f32[16]{0:T(128)S(1)}, f32[8,16,64,64]{3,2,1,0:T(8,128)}, f32[8,16]{1,0:T(8,128)S(1)}, /*index=5...) while((s32[]{:T(128)}, f32[16,64,64]{2,1,0:T(8,128)S(1)}, ...), condition=%wide.region_7.8_spmd.clone, body=%wide.region_6.7_spmd.clone.sunk | while | flops 262179 | bytes 1574005 | solution.py:184
  269.1 5.4 fusion.77
  276.9 16.6 %while.83 = (s32[]{:T(128)}, f32[16,64,64]{2,1,0:T(8,128)S(1)}, f32[16]{0:T(128)S(1)}, f32[8,16,64,64]{3,2,1,0:T(8,128)}, f32[8,16]{1,0:T(8,128)S(1)}, /*index=5...) while((s32[]{:T(128)}, f32[16,64,64]{2,1,0:T(8,128)S(1)}, ...), condition=%wide.region_11.12_spmd.clone, body=%wide.region_10.11_spmd.clone.sunk | while | flops 262180 | bytes 1573517 | solution.py:187
  294.4 5.4 copy.176
  299.8 2.9 copy.182
  305.2 5.3 copy.172
  310.5 2.9 copy.178
  313.8 13.8 %all-reduce.2 = (f32[128]{0:T(128)S(1)}, f32[128]{0:T(128)S(1)}) all-reduce(f32[128]{0:T(128)S(1)} %dynamic-update-slice, f32[128]{0:T(128)S(1)} %dynamic-update-slice.1), channel_id=2, replica_groups=mesh['tm'=8,'lane'=4] {'tm'}, use_global_device_ids=true, to_apply=%add | all-reduce | flops 256 | bytes 2048
  327.7 6.7 select_n.81
  334.6 8.5 %while.82 = (s32[]{:T(128)}, f32[16,64,64]{2,1,0:T(8,128)S(1)}, s32[]{:T(128)}, f32[8,16]{1,0:T(8,128)S(1)}, f32[8,16,64,64]{3,2,1,0:T(8,128)}, /*index=5*/s32[]{:T(128)}, s32[]{:T(128)}) while((s32[]{:T(128)}, f32[16,64,64]{2,1,0:T(8,128)S(1)}, s32[]{:T(128)}, f32[8,16]{1,0:T(8,128)S(1)}, f32[8,16,64,64]{3,2,1,0:T(8,128)}, ...), condition=%wide.region_9.10_spmd.clone, body=%wide.region_8.9_spmd.clone.sunk | while | flops 262148 | bytes 786729 | solution.py:30
  343.5 4.7 rev.7
  348.2 8.5 %while.84 = (s32[]{:T(128)}, f32[16,64,64]{2,1,0:T(8,128)S(1)}, s32[]{:T(128)}, f32[8,16]{1,0:T(8,128)S(1)}, f32[8,16,64,64]{3,2,1,0:T(8,128)}, /*index=5*/s32[]{:T(128)}, s32[]{:T(128)}) while((s32[]{:T(128)}, f32[16,64,64]{2,1,0:T(8,128)S(1)}, s32[]{:T(128)}, f32[8,16]{1,0:T(8,128)S(1)}, f32[8,16,64,64]{3,2,1,0:T(8,128)}, ...), condition=%wide.region_13.14_spmd.clone, body=%wide.region_12.13_spmd.clone.sunk | while | flops 262148 | bytes 786729 | solution.py:30
  356.7 5.4 multiply_add_fusion
  362.0 143.6 %while.80 = (s32[]{:T(128)}, bf16[8,256,1024]{2,1,0:T(8,128)(2,1)}, bf16[8,256,1024]{2,1,0:T(8,128)(2,1)}, bf16[8,256,128]{2,1,0:T(8,128)(2,1)S(1)}, bf16[8,256,...) while((s32[]{:T(128)}, bf16[8,256,1024]{2,1,0:T(8,128)(2,1)}, ...), condition=%wide.region_20.21_spmd, body=%wide.region_14.20_spmd.sunk | while | flops 582320192 | bytes 16335057 | solution.py:198
  374.1 2.7 convert_reduce_fusion.3
  392.1 2.7 convert_reduce_fusion.3
  410.0 2.7 convert_reduce_fusion.3
  427.9 2.7 convert_reduce_fusion.3
  445.9 2.7 convert_reduce_fusion.3
  463.9 2.7 convert_reduce_fusion.3
  481.8 2.7 convert_reduce_fusion.3
  499.8 2.7 convert_reduce_fusion.3
  505.7 8.2 %fusion.96 = f32[1024,1024]{0,1:T(8,128)S(1)} fusion(bf16[2048,1024]{1,0:T(8,128)(2,1)} %select_n.81, bf16[2048,1024]{1,0:T(8,128)(2,1)} %bitcast.316), kind=kOutput, calls=%fused_computation.159 | convolution fusion | flops 4294967296 | bytes 12582912 | tf_op jit(solution)/shard_map/dot_general | solution.py:223
  516.1 4.9 fusion.68
  521.0 4.0 maximum_multiply_fusion
  525.0 9.3 %copy.200 = f32[1024,2176]{1,0:T(8,128)} copy(f32[1024,2176]{0,1:T(8,128)} %maximum_multiply_fusion) | data formatting | bytes 17825792
  534.3 196.7 %reduce-scatter.4.cloned.1.call-done = f32[32,2176]{1,0:T(8,128)} async-done(((f32[1024,2176]{1,0:T(8,128)}), f32[32,2176]{1,0:T(8,128)}) %reduce-scatter.4.cloned.1.call-update) | async-done | bytes 278544
  (464 shorter events, 200.5 us)
Async XLA Ops:
  7.2 79.3 %copy-start = (bf16[1024,1024]{1,0:T(8,128)(2,1)S(1)}, bf16[1024,1024]{1,0:T(8,128)(2,1)}, u32[]{:S(2)}) copy-start(bf16[1024,1024]{1,0:T(8,128)(2,1)} %param.29) | copy-start | bytes 6291460
  8.3 0.7 copy-start.17
  68.7 6.5 copy-start.19
  68.7 7.9 %copy-start.13 = (s32[1,2048]{1,0:T(1,128)S(1)}, s32[1,2048]{1,0:T(1,128)}, u32[]{:S(2)}) copy-start(s32[1,2048]{1,0:T(1,128)} %param.25) | copy-start | bytes 24580
  68.7 9.9 %copy-start.12 = (f32[1,16,2048]{2,1,0:T(8,128)S(1)}, f32[1,16,2048]{2,1,0:T(8,128)}, u32[]{:S(2)}) copy-start(f32[1,16,2048]{2,1,0:T(8,128)} %param.24) | copy-start | bytes 393220
  68.7 99.9 %all-to-all-start = ((bf16[4,2,262144]{2,1,0:T(2,128)(2,1)}), bf16[4,2,262144]{2,1,0:T(2,128)(2,1)}, u32[]{:S(2)}, u32[]{:S(2)}) async-start(bf16[4,2,262144]{2,1,0:T(2,128)(2,1)} %reshape.387), calls=%async_computation | async-start | bytes 8388608 | tf_op jit(solution)/shard_map/all_to_all | solution.py:143
  75.2 259.4 %all-gather.7.cloned.1.call-start = ((), (), s32[]{:S(2)}) async-start(), calls=%async_computation.2 | async-start | bytes 4718592 | tf_op jit(solution)/shard_map/all_gather | solution.py:18
  85.0 0.7 copy-start.10
  101.5 6.5 copy-start.11
  217.6 6.2 copy-start.18
  217.6 6.2 copy-start.22
  238.9 3.8 copy-start.9
  238.9 3.9 copy-start.23
  242.7 2.2 copy-start.6
  245.8 3.2 copy-start.4
  249.1 2.5 copy-start.16
  268.2 0.8 copy-start.3
  269.0 74.5 %all-gather.9.cloned.1.call-start = ((), (), s32[]{:S(2)}) async-start(), calls=%async_computation.3 | async-start | bytes 4718592 | tf_op jit(solution)/shard_map/all_gather | solution.py:18
  274.5 2.4 copy-start.15
  293.5 0.8 copy-start.2
  294.3 436.7 %reduce-scatter.4.cloned.1.call-start = ((), (), s32[]{:S(2)}) async-start(), calls=%async_computation.4 | async-start | bytes 9191424
  294.4 5.4 copy-start.5
  299.8 3.5 copy-start.14
  299.8 4.1 copy-start.24
  305.2 5.3 copy-start.7
  505.7 8.2 %copy-start.8 = (bf16[2048,1024]{1,0:T(8,128)(2,1)S(1)}, bf16[2048,1024]{1,0:T(8,128)(2,1)}, u32[]{:S(2)}) copy-start(bf16[2048,1024]{1,0:T(8,128)(2,1)} %select_n.81) | copy-start | bytes 12582916
  505.7 9.0 %copy-start.21 = (bf16[8,256,1024]{2,1,0:T(8,128)(2,1)S(1)}, bf16[8,256,1024]{2,1,0:T(8,128)(2,1)}, u32[]{:S(2)}) copy-start(bf16[8,256,1024]{2,1,0:T(8,128)(2,1)} %get-tuple-element.471) | copy-start | bytes 12582916
  513.9 2.2 copy-start.20
  534.3 199.8 %copy-start.1 = (bf16[1024,1024]{1,0:T(8,128)(2,1)S(1)}, bf16[1024,1024]{1,0:T(8,128)(2,1)}, u32[]{:S(2)}) copy-start(bf16[1024,1024]{1,0:T(8,128)(2,1)} %param.29) | copy-start | bytes 6291460
Sparse Core Ops, SparseCore 0:
  269.1 35.7 all-gather.6
  306.8 36.6 all-gather.8
  534.5 196.5 reduce-scatter.3
where the time goes:
time: 752 us; the launch traced here: 741 us
  waiting for transfers between devices  253 us (34%)
  matrix products  159 us (21%)
  local copies, waits for them, and re-layouts  150 us (20%)
  other arithmetic  142 us (19%)
  between operations  15 us (2%)
  blocking collectives  13.8 us (2%)
    unnamed x4, waiting for transfers between devices  197 us
    dot_general x74, matrix products, product(): jnp.einsum(spec, left_op, right_op, preferred_element_type=jnp.float32)  113 us
    all_to_all x2, other arithmetic, on_device(): lax.all_to_all(outgoing.reshape(lane_count, capacity * BLOCK * D), 'lane'...  57.2 us
    all_to_all x1, waiting for transfers between devices, on_device(): lax.all_to_all(outgoing.reshape(lane_count, capacity * BLOCK * D), 'lane'...  55.5 us
    unnamed x64, local copies, waits for them, and re-layouts  39.8 us
    add x16, other arithmetic, advance(): block_factor[:, None, None] * current + pushed  18.5 us
    dynamic_update_slice x48, local copies, waits for them, and re-layouts, on_device(): lax.map(block_grads, (inner_b, write_b, read_b, upstream_b, rates_b, flag...  17.8 us
    select_n x14, other arithmetic, hop(): jnp.where(position < mine, new, old)  16.4 us
  transfers between devices with their start and end apart: 4, of which 3 were waited for; matrix products, arithmetic and copies ran while one was open for 13% of the time, Pallas kernels for 0%

commit v1 on v0

v1 whole, which is shorter than its diff:
```python
import math

import jax
import jax.numpy as jnp
from jax import lax
from jax.experimental import pallas as pl
from jax.experimental.pallas import tpu as pltpu
from jax.sharding import PartitionSpec as P

STATE = 64
BLOCK = 256
BUFCH = 4
F32 = jnp.float32
BF = jnp.bfloat16


def dot(a, b, ca, cb):
    return lax.dot_general(a, b, (((ca,), (cb,)), ((), ())), preferred_element_type=F32)


def split3(x):
    hi = x.astype(BF)
    rest = x - hi.astype(F32)
    mid = rest.astype(BF)
    low = (rest - mid.astype(F32)).astype(BF)
    return hi, mid, low


def decay_parts(rates, heads):
    a = lax.broadcasted_iota(jnp.int32, (BLOCK, BLOCK), 0)
    b = lax.broadcasted_iota(jnp.int32, (BLOCK, BLOCK), 1)
    lower = (b <= a).astype(F32).astype(BF)
    cum_col = 0.0
    cum_row = 0.0
    for part in split3(rates):
        cum_col = cum_col + dot(lower, part, 1, 1)
        cum_row = cum_row + dot(part, lower, 1, 1)
    cnt_col = cum_col[:, heads : heads + 1]
    cnt_row = cum_row[heads : heads + 1, :]
    cum = cum_col[:, :heads]
    last = cum_col[BLOCK - 1 : BLOCK, :]
    opening = jnp.where(cnt_col == 0.0, jnp.exp(cum), 0.0)
    closing = jnp.where(
        cnt_col == last[:, heads : heads + 1], jnp.exp(last[:, :heads] - cum), 0.0
    )
    linked = (cnt_col == cnt_row) & (b <= a)
    return cum, cum_row, opening, closing, linked


def widen(x, heads, width):
    a = lax.broadcasted_iota(jnp.int32, (heads, width), 0)
    b = lax.broadcasted_iota(jnp.int32, (heads, width), 1)
    per = width // heads
    spread = ((b >= a * per) & (b < (a + 1) * per)).astype(F32).astype(BF)
    total = 0.0
    for part in split3(x):
        total = total + dot(part, spread, 1, 0)
    return total


def pick_kernel(sel, src, out):
    out[...] = src[...]


def project_kernel(
    heads,
    pick,
    fill,
    recv,
    up,
    rates,
    w_in,
    w_bc,
    rows_o,
    inner_o,
    keys_o,
    push_f,
    push_b,
    fac,
):
    k = pl.program_id(0)
    pos = lax.broadcasted_iota(jnp.int32, recv.shape[1:], 0)
    rows = jnp.where(pos < fill[k], recv[0], jnp.zeros((), BF))
    rows_o[...] = rows
    inner = dot(rows, w_in[...], 1, 0).astype(BF)
    inner_o[...] = inner
    keys = dot(rows, w_bc[...], 1, 0).astype(BF)
    keys_o[...] = keys
    _, _, opening, closing, _ = decay_parts(rates[...], heads)
    width = inner.shape[1]
    open_w = widen(opening, heads, width)
    close_w = widen(closing, heads, width)
    w_inn = (close_w * inner.astype(F32)).astype(BF)
    w_out = (open_w * up[...].astype(F32)).astype(BF)
    push_f[0] = dot(keys, w_inn, 0, 0)[:STATE]
    push_b[0] = dot(keys, w_out, 0, 0)[STATE:]
    fac[0] = jnp.broadcast_to(open_w[BLOCK - 1 : BLOCK], fac.shape[1:])


def mix_kernel(heads, inner_r, up_r, keys_r, rates, st, fin, read_o, gin_o, gk_o, acc):
    inner = inner_r[...]
    up = up_r[...]
    keys = keys_r[...]
    width = inner.shape[1]
    per = width // heads
    write = keys[:, :STATE]
    read = keys[:, STATE:]
    cum, cum_row, opening, closing, linked = decay_parts(rates[...], heads)
    bias = jnp.where(linked, 0.0, -1e30)
    scores = dot(read, write, 1, 1)
    open_w = widen(opening, heads, width)
    close_w = widen(closing, heads, width)
    start = st[0]
    finish = fin[0]
    up_t = up.T
    lane = lax.broadcasted_iota(jnp.int32, (BLOCK, 2 * per), 1)
    first = lane < per
    zero = jnp.zeros((), BF)
    carried = open_w * dot(read, start, 1, 0)
    returned = close_w * dot(write, finish, 1, 0)
    for g in range(heads // 2):
        cols = slice(2 * g * per, 2 * (g + 1) * per)
        in_p = inner[:, cols]
        up_p = up[:, cols]
        outs = []
        backs = []
        for s in range(2):
            h = 2 * g + s
            decay = jnp.exp(cum[:, h : h + 1] - cum_row[h : h + 1, :] + bias)
            mixing = (decay * scores).astype(BF)
            pairing = dot(jnp.where(first == (s == 0), up_p, zero), in_p, 1, 1)
            if h == 0:
                acc[...] = decay * pairing
            else:
                acc[...] += decay * pairing
            outs.append(dot(mixing, in_p, 1, 0))
            backs.append(dot(up_t[h * per : (h + 1) * per], mixing, 1, 0))
        read_o[:, cols] = (jnp.where(first, outs[0], outs[1]) + carried[:, cols]).astype(BF)
        back = jnp.concatenate(backs, axis=0).T
        gin_o[:, cols] = (back + returned[:, cols]).astype(BF)
    blended = acc[...].astype(BF)
    w_inn = (close_w * inner.astype(F32)).astype(BF)
    w_out = (open_w * up.astype(F32)).astype(BF)
    gk_o[:, :STATE] = (dot(blended, read, 0, 0) + dot(w_inn, finish, 1, 1)).astype(BF)
    gk_o[:, STATE:] = (dot(blended, write, 1, 0) + dot(w_out, start, 1, 1)).astype(BF)


def on_device(
    replay, block_owner, block_slot, block_fill, log_decay, resets, cotangent, w_in, w_bc, w_out
):
    lane_count = lax.axis_size("lane")
    shards = lax.axis_size("tm")
    my_lane = lax.axis_index("lane")
    mine = lax.axis_index("tm")
    width = replay.shape[3]
    heads = log_decay.shape[1]
    blocks = block_fill.shape[2]
    tokens = cotangent.shape[1]
    owners = block_owner[0, :, :, 0]
    slot_map = block_slot[0]
    my_owner = lax.dynamic_index_in_dim(owners, my_lane, 0, keepdims=False)
    capacity = max(2, (blocks + lane_count - 1) // lane_count)
    order_pos = lax.broadcasted_iota(jnp.int32, (blocks, blocks), 0)
    other_pos = lax.broadcasted_iota(jnp.int32, (blocks, blocks), 1)
    ranking = jnp.sum(
        ((owners[:, :, None] == owners[:, None, :]) & (other_pos < order_pos)[None]).astype(
            jnp.int32
        ),
        axis=2,
    )
    slot_ids = lax.broadcasted_iota(jnp.int32, (lane_count, capacity, blocks), 1)
    picked = (owners[:, None, :] == my_lane) & (ranking[:, None, :] == slot_ids)
    chosen = jnp.sum(jnp.where(picked, slot_map[:, None, :], 0), axis=2).reshape(-1)
    slots = lane_count * capacity
    outgoing = pl.pallas_call(
        pick_kernel,
        name="pick",
        out_shape=jax.ShapeDtypeStruct((slots, BLOCK, width), BF),
        grid_spec=pltpu.PrefetchScalarGridSpec(
            num_scalar_prefetch=1,
            grid=(slots,),
            in_specs=[pl.BlockSpec((1, BLOCK, width), lambda i, s: (s[i], 0, 0))],
            out_specs=pl.BlockSpec((1, BLOCK, width), lambda i, s: (i, 0, 0)),
        ),
    )(chosen, replay.reshape(BUFCH, BLOCK, width))
    received = lax.all_to_all(outgoing, "lane", split_axis=0, concat_axis=0, tiled=True)
    my_rank = lax.dynamic_index_in_dim(ranking, my_lane, 0, keepdims=False)
    pick = my_owner * capacity + my_rank
    fill = block_fill[0, 0]
    usable = (lax.broadcasted_iota(jnp.int32, (blocks, BLOCK), 1) < fill[:, None]).reshape(tokens)
    masked = jnp.where(usable[:, None], cotangent[0], jnp.zeros((), BF))
    upstream = dot(masked, w_out, 1, 1).astype(BF)
    pad = (-(heads + 1)) % 8
    rates = jnp.concatenate(
        [log_decay[0], resets.astype(F32), jnp.zeros((pad, tokens), F32)], axis=0
    )
    rate_rows = heads + 1 + pad
    row_spec = pl.BlockSpec((BLOCK, width), lambda k, *s: (k, 0))
    key_spec = pl.BlockSpec((BLOCK, 2 * STATE), lambda k, *s: (k, 0))
    rate_spec = pl.BlockSpec((rate_rows, BLOCK), lambda k, *s: (0, k))
    state_spec = pl.BlockSpec((1, STATE, width), lambda k, *s: (k, 0, 0))
    row_shape = jax.ShapeDtypeStruct((tokens, width), BF)
    key_shape = jax.ShapeDtypeStruct((tokens, 2 * STATE), BF)
    state_shape = jax.ShapeDtypeStruct((blocks, STATE, width), F32)
    rows, inner, keys, push_f, push_b, fac = pl.pallas_call(
        lambda *a: project_kernel(heads, *a),
        name="project",
        out_shape=(
            row_shape,
            row_shape,
            key_shape,
            state_shape,
            state_shape,
            jax.ShapeDtypeStruct((blocks, 8, width), F32),
        ),
        grid_spec=pltpu.PrefetchScalarGridSpec(
            num_scalar_prefetch=2,
            grid=(blocks,),
            in_specs=[
                pl.BlockSpec((1, BLOCK, width), lambda k, p, f: (p[k], 0, 0)),
                row_spec,
                rate_spec,
                pl.BlockSpec((width, width), lambda k, *s: (0, 0)),
                pl.BlockSpec((width, 2 * STATE), lambda k, *s: (0, 0)),
            ],
            out_specs=(
                row_spec,
                row_spec,
                key_spec,
                state_spec,
                state_spec,
                pl.BlockSpec((1, 8, width), lambda k, *s: (k, 0, 0)),
            ),
        ),
    )(pick, fill, received, upstream, rates, w_in, w_bc)
    factor = fac[:, :1]

    def sweep(order, push):
        state = jnp.zeros((STATE, width), F32)
        gain = jnp.ones((1, width), F32)
        states = [None] * blocks
        gains = [None] * blocks
        for k in order:
            states[k], gains[k] = state, gain
            state = factor[k] * state + push[k]
            gain = gain * factor[k]
        return state, gain, states, gains

    fwd = sweep(range(blocks), push_f)
    bwd = sweep(range(blocks - 1, -1, -1), push_b)
    packet = jnp.concatenate([fwd[0], bwd[0], jnp.broadcast_to(fwd[1], (8, width))], axis=0)
    pieces = lax.all_gather(packet, "tm")
    enter = jnp.zeros((STATE, width), F32)
    adjoint = jnp.zeros((STATE, width), F32)
    for s in range(shards - 1):
        r = shards - 1 - s
        enter = jnp.where(
            s < mine, pieces[s, 2 * STATE : 2 * STATE + 1] * enter + pieces[s, :STATE], enter
        )
        adjoint = jnp.where(
            r > mine,
            pieces[r, 2 * STATE : 2 * STATE + 1] * adjoint + pieces[r, STATE : 2 * STATE],
            adjoint,
        )
    starts = jnp.stack([(a + b * enter).astype(BF) for a, b in zip(fwd[2], fwd[3])])
    ends = jnp.stack([(a + b * adjoint).astype(BF) for a, b in zip(bwd[2], bwd[3])])
    readout, grad_inner, grad_keys = pl.pallas_call(
        lambda *a: mix_kernel(heads, *a),
        name="mix",
        out_shape=(row_shape, row_shape, key_shape),
        grid=(blocks,),
        in_specs=[row_spec, row_spec, key_spec, rate_spec, state_spec, state_spec],
        out_specs=(row_spec, row_spec, key_spec),
        scratch_shapes=[pltpu.VMEM((BLOCK, BLOCK), F32)],
    )(inner, upstream, keys, rates, starts, ends)
    devices = shards * lane_count
    grad_scale = 1.0 / math.sqrt(tokens * devices)

    def collect(terms):
        part = lax.all_to_all(
            terms.astype(BF), ("tm", "lane"), split_axis=0, concat_axis=0, tiled=True
        )
        part = part.reshape(devices, part.shape[0] // devices, part.shape[1])
        return jnp.sum(part.astype(F32), axis=0) * grad_scale

    g_out = collect(dot(readout, masked, 0, 0))
    g_in = collect(
        jnp.concatenate([dot(rows, grad_inner, 0, 0), dot(rows, grad_keys, 0, 0)], axis=1)
    )
    return (g_in[:, :width], g_in[:, width:], g_out)


def solution(mesh):
    placed = (
        P("lane", "tm", None, None),
        P("tm", None, None, None),
        P("tm", None, None),
        P("lane", "tm", None),
        P("lane", None, "tm"),
        P("lane", "tm"),
        P("lane", "tm", None),
        P(),
        P(),
        P(),
    )
    return jax.shard_map(
        on_device,
        mesh=mesh,
        in_specs=placed,
        out_specs=(P(("tm", "lane"), None), P(("tm", "lane"), None), P(("tm", "lane"), None)),
        check_vma=False,
    )
```

time: 752 us -> 358 us (0.48); the launches traced: 741 us -> 356 us
  local copies, waits for them, and re-layouts: 150 us -> 4.91 us
  matrix products: 159 us -> 28.7 us
  other arithmetic: 142 us -> 27 us
  Pallas kernels: 0 us -> 60.1 us
  waiting for transfers between devices: 253 us -> 204 us
  blocking collectives: 13.8 us -> 0 us
  starting transfers between devices: 6.56 us -> 16.4 us
    unnamed x4 -> x1, waiting for transfers between devices: 197 us -> 0.02 us
    dot_general x90 -> x4, matrix products: 159 us -> 28.7 us  [dot(): lax.dot_general(a, b, (((ca,), (cb,)), ((), ())), preferred_element_type=...]
    all_to_all x1 -> x3, waiting for transfers between devices: 55.5 us -> 167 us  [the longest x2 84.5 us: collect(): lax.all_to_all(terms.astype(BF), ('tm', 'lane'), split_axis=0, concat_axi...]
    pallas_call x0 -> x3, Pallas kernels: none -> 60.1 us  [the longest x1 30.4 us: on_device(): pl.pallas_call(lambda *a: mix_kernel(heads, *a), name='mix', out_shape=(r...]
    all_to_all x2 -> x0, other arithmetic: 57.2 us -> none  [on_device(): lax.all_to_all(outgoing.reshape(lane_count, capacity * BLOCK * D), 'lane'...]
    unnamed x64 -> x20, local copies, waits for them, and re-layouts: 39.8 us -> 1.95 us
    all_gather x2 -> x1, waiting for transfers between devices: 0.46 us -> 37.2 us  [on_device(): pieces = lax.all_gather(packet, 'tm')]
    convert_element_type x4 -> x0, local copies, waits for them, and re-layouts: 23.7 us -> none  [the longest x1 6.52 us: on_device(): upstream = lax.dot_general(masked, w_out, (((1,), (1,)), ((), ())), prefe...]
  transfers between devices with their start and end apart: 4 -> 4, of which waited for: 3 -> 4; matrix products, arithmetic and copies ran while one was open for 13% -> 7% of each run, Pallas kernels for 0% -> 0%
where the time goes in v1:
time: 358 us; the launch traced here: 356 us
  waiting for transfers between devices  204 us (57%)
  Pallas kernels  60.1 us (17%)
  matrix products  28.7 us (8%)
  other arithmetic  27 us (8%)
  starting transfers between devices  16.4 us (5%)
  between operations  14.3 us (4%)
  local copies, waits for them, and re-layouts  4.91 us (1%)
    all_to_all x2, waiting for transfers between devices, collect(): lax.all_to_all(terms.astype(BF), ('tm', 'lane'), split_axis=0, concat_axi...  84.5 us
    all_to_all x1, waiting for transfers between devices, on_device(): lax.all_to_all(outgoing, 'lane', split_axis=0, concat_axis=0, tiled=True)  82.5 us
    all_gather x1, waiting for transfers between devices, on_device(): pieces = lax.all_gather(packet, 'tm')  37.2 us
    pallas_call x1, Pallas kernels, on_device(): pl.pallas_call(lambda *a: mix_kernel(heads, *a), name='mix', out_shape=(r...  30.4 us
    dot_general x4, matrix products, dot(): lax.dot_general(a, b, (((ca,), (cb,)), ((), ())), preferred_element_type=...  28.7 us
    pallas_call x1, Pallas kernels, on_device(): pl.pallas_call(lambda *a: project_kernel(heads, *a), name='project', out_...  22.8 us
    unnamed x11, other arithmetic  9.8 us
    all_to_all x2, starting transfers between devices, collect(): lax.all_to_all(terms.astype(BF), ('tm', 'lane'), split_axis=0, concat_axi...  9.41 us
  transfers between devices with their start and end apart: 4, of which 4 were waited for; matrix products, arithmetic and copies ran while one was open for 7% of the time, Pallas kernels for 0%

profile of v1, /device:TPU:0, one launch (start us, length us, event | category | flops | bytes accessed | tf_op | source)
XLA Modules:
  0.0 355.6 jit_solution(8571360013262923766)
XLA Ops:
  7.2 0.0 copy-start
  7.2 1.1 convert_reduce_fusion.2
  8.3 0.7 broadcast_compare_fusion
  8.9 0.8 select_reduce_fusion
  9.8 0.1 copy.13
  9.9 0.6 reshape.1385.sel
  10.5 6.9 %pick.1 = bf16[8,256,1024]{2,1,0:T(8,128)(2,1)} custom-call(s32[8]{0:T(128)} %reshape.1385.sel, bf16[4,256,1024]{2,1,0:T(8,128)(2,1)} %bitcast.130), custom_call_target="tpu_custom_call" | custom-call | tf_op jit(solution)/shard_map/pick/pallas_call | solution.py:175
  17.4 7.0 %all-to-all-start = ((bf16[8,256,1024]{2,1,0:T(8,128)(2,1)}), bf16[8,256,1024]{2,1,0:T(8,128)(2,1)}, u32[]{:S(2)}, u32[]{:S(2)}) async-start(bf16[8,256,1024]{2,1,0:T(8,128)(2,1)} %pick.1), calls=%async_computation | async-start | bytes 8388608 | tf_op jit(solution)/shard_map/all_to_all | solution.py:186
  24.4 0.1 iota_compare_fusion
  24.5 0.1 pad.7.clone
  24.6 1.2 bitcast_add_fusion.16.a_0_
  25.8 0.8 maximum_maximum_fusion.a_4_.a_3_
  26.5 8.6 %convolution_convert_fusion.a_3_.a_1_ = bf16[2048,1024]{1,0:T(8,128)(2,1)} fusion(bf16[1024,1024]{1,0:T(8,128)(2,1)S(1)} %copy-done, bf16[1,2048,1024]{2,1,0:T(8,128)(2,1)} %param.16, pred[2048]{0:T(1024)(128)(4,1)S(1)} %lt.52), kind=kOutput, calls=%fused_computation.3 | convolution fusion | flops 4299161600 | bytes 10487808 | tf_op jit(solution)/shard_map/dot_general | solution.py:18
  35.2 82.5 %all-to-all-done.a_2_ = bf16[8,256,1024]{2,1,0:T(8,128)(2,1)} async-done(((bf16[8,256,1024]{2,1,0:T(8,128)(2,1)}), bf16[8,256,1024]{2,1,0:T(8,128)(2,1)}, u32[]{:S(2)}, u32[]{:S(2)}) %all-to-all-start) | async-done | bytes 4194336 | tf_op jit(solution)/shard_map/all_to_all | solution.py:186
  117.6 22.8 %project.1 = (bf16[2048,1024]{1,0:T(8,128)(2,1)}, bf16[2048,1024]{1,0:T(8,128)(2,1)}, bf16[2048,128]{1,0:T(8,128)(2,1)}, f32[8,64,1024]{2,1,0:T(8,128)}, f32[8,64,1024]{2,1,0:T(8,128)}, /*index=5*/f32[8,8,1024]{2,1,0:T(8,128)}) custom-call(s32[8]{0:T(128)} %bitcast_add_fusion.16.a_0_, s32[8]{0:T(128)} %bitcast.188, bf16[8,256,1024]{2,1,0:T(8,128)(2,1)} %all-to-all-done.a_2_, ...), custom_call_target="tpu_custom_call" | custom-call | tf_op jit(solution)/shard_map/project/pallas_call | solution.py:205
  140.5 0.9 fusion.49
  141.4 1.7 bitcast_add_fusion.8
  143.1 1.7 bitcast_add_fusion
  144.8 0.9 pad_maximum_fusion.1
  145.7 0.0 all-gather.3.cloned.1.call-update
  145.8 37.2 %all-gather.3.cloned.1.call-done = f32[1088,1024]{1,0:T(8,128)} async-done(((f32[136,1024]{1,0:T(8,128)}), f32[1088,1024]{1,0:T(8,128)}) %all-gather.3.cloned.1.call-update) | async-done | bytes 4456464 | tf_op jit(solution)/shard_map/all_gather | solution.py:252
  183.0 0.9 slice_multiply_fusion
  183.9 1.6 convert_dynamic-update-slice_fusion.1
  185.5 1.1 fusion.28
  186.6 1.1 fusion.29
  187.7 1.0 fusion.30
  188.8 2.5 fusion.35
  191.3 1.1 fusion.31
  192.5 0.1 fusion.32
  192.6 1.1 fusion.33
  193.7 1.1 fusion.34
  194.8 1.0 copy-done.4
  195.8 1.0 copy-done.3
  196.7 30.4 %mix.1 = (bf16[2048,1024]{1,0:T(8,128)(2,1)}, bf16[2048,1024]{1,0:T(8,128)(2,1)}, bf16[2048,128]{1,0:T(8,128)(2,1)}) custom-call(bf16[2048,1024]{1,0:T(8,128)(2,1)} %get-tuple-element.13.a_0_, bf16[2048,1024]{1,0:T(8,128)(2,1)} %convolution_convert_fusion.a_3_.a_1_, bf16[2048,128]{1,0:T(8,128)(2,1)} %get-tuple-element.14.a_2_, ...), custom_call_target="tpu_custom_call" | custom-call | tf_op jit(solution)/shard_map/mix/pallas_call | solution.py:267
  227.1 9.5 %convolution_convert_fusion.1 = bf16[1024,1024]{1,0:T(8,128)(2,1)} fusion(bf16[2048,1024]{1,0:T(8,128)(2,1)} %get-tuple-element.20, bf16[1,2048,1024]{2,1,0:T(8,128)(2,1)} %param.16, pred[2048]{0:T(1024)(128)(4,1)S(1)} %lt.52), kind=kOutput, calls=%fused_computation.5 | convolution fusion | flops 4298113024 | bytes 10487808 | tf_op jit(solution)/shard_map/dot_general | solution.py:18
  236.6 4.7 %all-to-all-start.2 = ((bf16[32,32,1024]{2,1,0:T(8,128)(2,1)}), bf16[32,32,1024]{2,1,0:T(8,128)(2,1)}, u32[]{:S(2)}, u32[]{:S(2)}) async-start(bf16[32,32,1024]{2,1,0:T(8,128)(2,1)} %bitcast.43), calls=%async_computation.2 | async-start | bytes 4194304 | tf_op jit(solution)/shard_map/all_to_all | solution.py:280
  241.3 3.6 %convolution_convert_fusion.3 = bf16[1024,128]{1,0:T(8,128)(2,1)S(1)} fusion(bf16[2048,1024]{1,0:T(8,128)(2,1)} %get-tuple-element.12, bf16[2048,128]{1,0:T(8,128)(2,1)S(1)} %copy-done.9), kind=kOutput, calls=%fused_computation.7 | convolution fusion | flops 537001984 | bytes 4980736 | tf_op jit(solution)/shard_map/dot_general | solution.py:18
  245.0 7.0 %convolution_convert_fusion.2 = bf16[1024,1024]{1,0:T(8,128)(2,1)S(1)} fusion(bf16[2048,1024]{1,0:T(8,128)(2,1)S(1)} %copy-done.8, bf16[2048,1024]{1,0:T(8,128)(2,1)} %get-tuple-element.18), kind=kOutput, calls=%fused_computation.6 | convolution fusion | flops 4296015872 | bytes 10485760 | tf_op jit(solution)/shard_map/dot_general | solution.py:18
  251.9 0.0 copy-start.1
  252.0 1.7 pad_maximum_fusion
  253.6 34.5 %all-to-all-done.2 = bf16[32,32,1024]{2,1,0:T(8,128)(2,1)} async-done(((bf16[32,32,1024]{2,1,0:T(8,128)(2,1)}), bf16[32,32,1024]{2,1,0:T(8,128)(2,1)}, u32[]{:S(2)}, u32[]{:S(2)}) %all-to-all-start.2) | async-done | bytes 2097184 | tf_op jit(solution)/shard_map/all_to_all | solution.py:280
  288.2 4.7 %all-to-all-start.1 = ((bf16[32,32,1152]{2,1,0:T(8,128)(2,1)}), bf16[32,32,1152]{2,1,0:T(8,128)(2,1)}, u32[]{:S(2)}, u32[]{:S(2)}) async-start(bf16[32,32,1152]{2,1,0:T(8,128)(2,1)} %pad_maximum_fusion), calls=%async_computation.1 | async-start | bytes 4718592 | tf_op jit(solution)/shard_map/all_to_all | solution.py:280
  292.9 2.0 convert_reduce_fusion.1
  294.8 0.7 broadcast_multiply_fusion.1
  295.5 50.0 %all-to-all-done.1 = bf16[32,32,1152]{2,1,0:T(8,128)(2,1)} async-done(((bf16[32,32,1152]{2,1,0:T(8,128)(2,1)}), bf16[32,32,1152]{2,1,0:T(8,128)(2,1)}, u32[]{:S(2)}, u32[]{:S(2)}) %all-to-all-start.1) | async-done | bytes 2359328 | tf_op jit(solution)/shard_map/all_to_all | solution.py:280
  345.4 2.0 convert_reduce_fusion
  347.5 0.7 slice.252
  348.1 0.6 slice.253
  (28 shorter events, 0.2 us)
Async XLA Ops:
  7.2 19.4 %copy-start = (bf16[1024,1024]{1,0:T(8,128)(2,1)S(1)}, bf16[1024,1024]{1,0:T(8,128)(2,1)}, u32[]{:S(2)}) copy-start(bf16[1024,1024]{1,0:T(8,128)(2,1)} %param.19) | copy-start | bytes 6291460
  17.4 7.0 %copy-start.7 = (s32[1,1,8]{2,1,0:T(1,128)S(1)}, s32[1,1,8]{2,1,0:T(1,128)}, u32[]{:S(2)}) copy-start(s32[1,1,8]{2,1,0:T(1,128)} %param.13) | copy-start | bytes 100
  17.4 7.1 %copy-start.6 = (s32[1,2048]{1,0:T(1,128)S(1)}, s32[1,2048]{1,0:T(1,128)}, u32[]{:S(2)}) copy-start(s32[1,2048]{1,0:T(1,128)} %param.15) | copy-start | bytes 24580
  17.4 8.4 %copy-start.5 = (f32[1,16,2048]{2,1,0:T(8,128)S(1)}, f32[1,16,2048]{2,1,0:T(8,128)}, u32[]{:S(2)}) copy-start(f32[1,16,2048]{2,1,0:T(8,128)} %param.14) | copy-start | bytes 393220
  17.4 100.3 %all-to-all-start = ((bf16[8,256,1024]{2,1,0:T(8,128)(2,1)}), bf16[8,256,1024]{2,1,0:T(8,128)(2,1)}, u32[]{:S(2)}, u32[]{:S(2)}) async-start(bf16[8,256,1024]{2,1,0:T(8,128)(2,1)} %pick.1), calls=%async_computation | async-start | bytes 8388608 | tf_op jit(solution)/shard_map/all_to_all | solution.py:186
  24.4 158.6 %all-gather.3.cloned.1.call-start = ((), (), s32[]{:S(2)}) async-start(), calls=%async_computation.3 | async-start | bytes 5013504 | tf_op jit(solution)/shard_map/all_gather | solution.py:252
  185.5 5.8 %copy-start.2 = (f32[8,64,1024]{2,1,0:T(8,128)S(1)}, f32[8,64,1024]{2,1,0:T(8,128)}, u32[]{:S(2)}) copy-start(f32[8,64,1024]{2,1,0:T(8,128)} %get-tuple-element.16) | copy-start | bytes 6291460
  194.8 1.0 copy-start.4
  195.8 1.0 copy-start.3
  236.6 4.8 %copy-start.9 = (bf16[2048,128]{1,0:T(8,128)(2,1)S(1)}, bf16[2048,128]{1,0:T(8,128)(2,1)}, u32[]{:S(2)}) copy-start(bf16[2048,128]{1,0:T(8,128)(2,1)} %get-tuple-element.19) | copy-start | bytes 1572868
  236.6 51.6 %all-to-all-start.2 = ((bf16[32,32,1024]{2,1,0:T(8,128)(2,1)}), bf16[32,32,1024]{2,1,0:T(8,128)(2,1)}, u32[]{:S(2)}, u32[]{:S(2)}) async-start(bf16[32,32,1024]{2,1,0:T(8,128)(2,1)} %bitcast.43), calls=%async_computation.2 | async-start | bytes 4194304 | tf_op jit(solution)/shard_map/all_to_all | solution.py:280
  241.3 3.7 %copy-start.8 = (bf16[2048,1024]{1,0:T(8,128)(2,1)S(1)}, bf16[2048,1024]{1,0:T(8,128)(2,1)}, u32[]{:S(2)}) copy-start(bf16[2048,1024]{1,0:T(8,128)(2,1)} %get-tuple-element.12) | copy-start | bytes 12582916
  251.9 96.8 %copy-start.1 = (bf16[1024,1024]{1,0:T(8,128)(2,1)S(1)}, bf16[1024,1024]{1,0:T(8,128)(2,1)}, u32[]{:S(2)}) copy-start(bf16[1024,1024]{1,0:T(8,128)(2,1)} %param.19) | copy-start | bytes 6291460
  288.2 57.3 %all-to-all-start.1 = ((bf16[32,32,1152]{2,1,0:T(8,128)(2,1)}), bf16[32,32,1152]{2,1,0:T(8,128)(2,1)}, u32[]{:S(2)}, u32[]{:S(2)}) async-start(bf16[32,32,1152]{2,1,0:T(8,128)(2,1)} %pad_maximum_fusion), calls=%async_computation.1 | async-start | bytes 4718592 | tf_op jit(solution)/shard_map/all_to_all | solution.py:280
Sparse Core Ops, SparseCore 0:
  145.8 37.0 all-gather.2
